TPU v7x, 512 devices: a whole 4x4x16 slice. The times are simulated.
512 devices in a mesh: mp: 2 (over y_hi), tok: 8 (over x, core), lat: 32 (over z, y_lo).
Axes of the slice: x: 4, y: 4 (y_hi: 2, y_lo: 2; y = y_hi * 2 + y_lo), z: 16, core: 2. Of those that a mesh axis runs over, the one named last changes fastest.
Arguments:
- inputs: bfloat16 [2, 384, 4608], P('mp', 'lat', 'tok'), may hold values from -6 to 6
- gate_w: bfloat16 [2, 4608, 18432], P('mp', 'tok', 'lat'), may hold values from -0.09375 to 0.09375
- up_w: bfloat16 [2, 4608, 18432], P('mp', 'tok', 'lat'), may hold values from -0.09375 to 0.09375
- down_w: bfloat16 [2, 18432, 4608], P('mp', 'lat', 'tok'), may hold values from -0.046875 to 0.046875
- enc_w: bfloat16 [2, 4608, 8192], P('mp', 'tok', 'lat'), may hold values from -0.0625 to 0.0625
- enc_bias: float32 [8192], P('lat'), may hold values from -3 to 3
- dec_w: bfloat16 [8192, 2, 4608], P('lat', 'mp', 'tok'), may hold values from -0.0625 to 0.0625
- dec_bias: float32 [2, 4608], P('mp', 'tok'), may hold values from -3 to 3
Outputs:
- recon_error: float32 [2, 384, 4608], P('mp', 'lat', 'tok')
- dec_grad: float32 [8192, 2, 4608], P('lat', 'mp', 'tok')
- latent_grad: float32 [384, 8192], P(None, 'lat')
All inputs are finite; a program needn't handle non-finite values.
Results may differ from a plain program's by a relative error of at most 0.009.
Values may be sent and summed in bfloat16 or wider, within the bound.
A program may use at most 64 MiB of HBM per device.

v0:
```python
import jax
import jax.numpy as jnp
from jax import lax
from jax.sharding import PartitionSpec as P


def contract_rows(left, right):
    return lax.dot_general(
        left, right, (((0,), (0,)), ((), ())), preferred_element_type=jnp.float32
    )


def contract_cols(left, right):
    return lax.dot_general(
        left, right, (((1,), (1,)), ((), ())), preferred_element_type=jnp.float32
    )


def body(inputs, gate_w, up_w, down_w, enc_w, enc_bias, dec_w, dec_bias):
    x_rows = inputs[0]
    gathered = lax.all_gather(x_rows, "lat", axis=0, tiled=True)
    gate_local = gate_w[0]
    up_local = up_w[0]
    width = gate_local.shape[1]
    block = gathered
    both = lax.psum_scatter(
        jnp.concatenate(
            [
                jnp.dot(block, gate_local, preferred_element_type=jnp.float32),
                jnp.dot(block, up_local, preferred_element_type=jnp.float32),
            ],
            axis=1,
        ),
        "tok",
        scatter_dimension=0,
        tiled=True,
    )
    hidden = (jax.nn.gelu(both[:, :width], approximate=True) * both[:, width:]).astype(jnp.bfloat16)
    hidden_all = lax.all_gather(hidden, "tok", axis=0, tiled=True)
    down_local = down_w[0]
    block = hidden_all
    acts = lax.psum_scatter(
        jnp.dot(block, down_local, preferred_element_type=jnp.float32),
        "lat",
        scatter_dimension=0,
        tiled=True,
    ).astype(jnp.bfloat16)
    acts_all = lax.all_gather(acts, "lat", axis=0, tiled=True)
    partial_pre = jnp.dot(acts_all, enc_w[0], preferred_element_type=jnp.float32)
    pre = lax.psum(partial_pre, ("mp", "tok"))
    codes = jnp.maximum(pre + enc_bias, 0.0).astype(jnp.bfloat16)
    decoder = dec_w[:, 0, :]
    bias_row = dec_bias[0]
    block = codes
    recon = lax.psum_scatter(
        jnp.dot(block, decoder, preferred_element_type=jnp.float32),
        "lat",
        scatter_dimension=0,
        tiled=True,
    )
    error = recon + bias_row - acts.astype(jnp.float32)
    error_all = lax.all_gather(error.astype(jnp.bfloat16), "lat", axis=0, tiled=True)
    decoder_grad = contract_rows(codes, error_all)
    latent_grad = lax.psum(contract_cols(error_all, decoder), ("mp", "tok"))
    return (error[None], decoder_grad[:, None, :], latent_grad)


def solution(mesh):
    in_specs = (
        P("mp", "lat", "tok"),
        P("mp", "tok", "lat"),
        P("mp", "tok", "lat"),
        P("mp", "lat", "tok"),
        P("mp", "tok", "lat"),
        P("lat"),
        P("lat", "mp", "tok"),
        P("mp", "tok"),
    )
    out_specs = (P("mp", "lat", "tok"), P("lat", "mp", "tok"), P(None, "lat"))
    return jax.shard_map(body, mesh=mesh, in_specs=in_specs, out_specs=out_specs, check_vma=False)
```

profile of v0, /device:TPU:1, one launch (start us, length us, event | category | flops | bytes accessed | tf_op | source)
XLA Modules:
  0.0 789.7 jit_solution(4947730989583786598)
XLA Ops:
  8.0 61.9 %all-gather = bf16[1,384,576]{2,0,1:T(2,128)(2,1)S(1)} all-gather(bf16[1,12,576]{2,0,1:T(2,128)(2,1)S(1)} %copy.20), channel_id=2, replica_groups=mesh['mp'=2,'tok'=8,'lat'=32] {'lat'}, dimensions={1}, use_global_device_ids=true | all-gather | bytes 456192 | tf_op jit(solution)/shard_map/all_gather | solution.py:21
  72.1 2.0 copy.25
  74.1 47.7 %reduce-scatter.8.cloned.1.call-done = f32[48,1152]{1,0:T(8,128)} async-done(((f32[384,1152]{1,0:T(8,128)}), f32[48,1152]{1,0:T(8,128)}) %reduce-scatter.8.cloned.1.call-update) | async-done | bytes 221200 | tf_op jit(solution)/shard_map/reduce_scatter | solution.py:26
  121.8 1.1 fusion.24
  122.9 15.4 %all_gather.13 = bf16[384,576]{1,0:T(8,128)(2,1)S(1)} all-gather(bf16[48,576]{1,0:T(8,128)(2,1)S(1)} %fusion.24), channel_id=1, replica_groups=mesh['mp'=2,'tok'=8,'lat'=32] {'tok'}, dimensions={0}, use_global_device_ids=true | all-gather | bytes 497664 | tf_op jit(solution)/shard_map/all_gather | solution.py:39
  138.8 59.0 %fusion = f32[16,576]{1,0:T(8,128)S(1)} fusion(f32[384,576]{1,0:T(8,128)S(1)} %fusion.2), kind=kCustom, calls=%all-reduce-scatter | all-reduce-scatter fusion | flops 294913 | bytes 923648
  197.9 1.7 collective-permute-start
  199.6 2.1 collective-permute-start.1
  201.7 6.0 collective-permute-start.7
  207.7 4.9 collective-permute-start.2
  212.7 4.9 collective-permute-start.3
  217.6 2.1 collective-permute-start.4
  219.8 3.5 collective-permute-start.5
  223.2 2.8 collective-permute-start.6
  226.1 1.3 dynamic-slice.6
  228.1 1.3 concatenate.4
  229.4 49.4 %all-gather.1 = bf16[32,12,576]{2,1,0:T(8,128)(2,1)S(1)} all-gather(bf16[1,12,576]{2,1,0:T(8,128)(2,1)S(1)} %fusion.31), channel_id=1, replica_groups=mesh['mp'=2,'tok'=8,'lat'=32] {'lat'}, dimensions={0}, use_global_device_ids=true | all-gather | bytes 456192 | tf_op jit(solution)/shard_map/all_gather | solution.py:48
  280.2 180.0 %all-reduce.7.cloned.1.call-done = f32[384,256]{1,0:T(8,128)} async-done(((f32[384,256]{1,0:T(8,128)}), f32[384,256]{1,0:T(8,128)}) %all-reduce.7.cloned.1.call-update) | async-done | bytes 393232 | tf_op jit(solution)/shard_map/psum | solution.py:50
  460.2 1.3 fusion.12
  461.6 59.2 %fusion.1 = f32[16,576]{1,0:T(8,128)S(1)} fusion(f32[384,576]{1,0:T(8,128)S(1)} %fusion.12), kind=kCustom, calls=%all-reduce-scatter.1 | all-reduce-scatter fusion | flops 294913 | bytes 923648
  520.7 1.3 collective-permute-start.10
  522.0 3.4 collective-permute-start.11
  525.5 7.0 collective-permute-start.15
  532.6 4.5 collective-permute-start.12
  537.1 3.9 collective-permute-start.13
  541.0 2.9 collective-permute-start.14
  543.9 3.1 collective-permute-start.8
  547.0 2.2 collective-permute-start.9
  551.3 48.9 %all-gather.2 = bf16[32,12,576]{2,1,0:T(8,128)(2,1)S(1)} all-gather(bf16[1,12,576]{2,1,0:T(8,128)(2,1)S(1)} %get-tuple-element.18), channel_id=1, replica_groups=mesh['mp'=2,'tok'=8,'lat'=32] {'lat'}, dimensions={0}, use_global_device_ids=true | all-gather | bytes 456192 | tf_op jit(solution)/shard_map/all_gather | solution.py:62
  602.2 1.2 convolution_bitcast_fusion
  603.3 178.1 %all-reduce.9.cloned.1.call-done = f32[384,256]{1,0:T(8,128)} async-done(((f32[384,256]{1,0:T(8,128)}), f32[384,256]{1,0:T(8,128)}) %all-reduce.9.cloned.1.call-update) | async-done | bytes 393232 | tf_op jit(solution)/shard_map/psum | solution.py:64
  781.4 1.8 copy.29
  (56 shorter events, 9.1 us)
Async XLA Ops:
  7.2 63.5 %copy-start = (bf16[1,576,576]{2,1,0:T(8,128)(2,1)S(1)}, bf16[1,576,576]{2,1,0:T(8,128)(2,1)}, u32[]{:S(2)}) copy-start(bf16[1,576,576]{2,1,0:T(8,128)(2,1)} %param.10) | copy-start | bytes 1990660
  7.2 114.6 %reduce-scatter.8.cloned.1.call-start = ((), (), s32[]{:S(2)}) async-start(), calls=%async_computation.3 | async-start | bytes 1990656 | tf_op jit(solution)/shard_map/reduce_scatter | solution.py:26
  70.0 1.3 copy-start.3
  74.0 64.2 %copy-start.4 = (bf16[1,576,576]{2,1,0:T(8,128)(2,1)S(1)}, bf16[1,576,576]{2,1,0:T(8,128)(2,1)}, u32[]{:S(2)}) copy-start(bf16[1,576,576]{2,1,0:T(8,128)(2,1)} %param.11) | copy-start | bytes 1990660
  74.1 386.2 %all-reduce.7.cloned.1.call-start = ((), (), s32[]{:S(2)}) async-start(), calls=%async_computation.1 | async-start | bytes 786432 | tf_op jit(solution)/shard_map/psum | solution.py:50
  138.8 140.3 %copy-start.5 = (bf16[1,576,256]{2,1,0:T(8,128)(2,1)S(1)}, bf16[1,576,256]{2,1,0:T(8,128)(2,1)}, u32[]{:S(2)}) copy-start(bf16[1,576,256]{2,1,0:T(8,128)(2,1)} %param.12) | copy-start | bytes 884740
  197.9 21.9 %collective-permute-start = (bf16[16,576]{1,0:T(8,128)(2,1)S(1)}, bf16[16,576]{1,0:T(8,128)(2,1)S(1)}, u32[]{:S(2)}, u32[]{:S(2)}) collective-permute-start(bf16[16,576]{1,0:T(8,128)(2,1)S(1)} %convert.14), channel_id=1, source_target_pairs={{0,1},{1,2},{2,3},{3,4},{4,5},{5,6},{6,7},{7,8},{8,9},{9,10},{10,1... | collective-permute-start | bytes 55304
  199.6 23.6 %collective-permute-start.1 = (bf16[16,576]{1,0:T(8,128)(2,1)S(1)}, bf16[16,576]{1,0:T(8,128)(2,1)S(1)}, u32[]{:S(2)}, u32[]{:S(2)}) collective-permute-start(bf16[16,576]{1,0:T(8,128)(2,1)S(1)} %convert.14), channel_id=1, source_target_pairs={{0,2},{1,3},{2,4},{3,5},{4,6},{5,7},{6,8},{7,9},{8,10},{9,11},{10,... | collective-permute-start | bytes 55304
  201.7 15.9 %collective-permute-start.7 = (bf16[12,576]{1,0:T(8,128)(2,1)S(1)}, bf16[12,576]{1,0:T(8,128)(2,1)S(1)}, u32[]{:S(2)}, u32[]{:S(2)}) collective-permute-start(bf16[12,576]{1,0:T(8,128)(2,1)S(1)} %slice.10), channel_id=1, source_target_pairs={{0,8},{1,9},{2,10},{3,11},{4,12},{5,13},{6,14},{7,15},{8,16},{9,17... | collective-permute-start | bytes 41480
  207.7 20.3 %collective-permute-start.2 = (bf16[16,576]{1,0:T(8,128)(2,1)S(1)}, bf16[16,576]{1,0:T(8,128)(2,1)S(1)}, u32[]{:S(2)}, u32[]{:S(2)}) collective-permute-start(bf16[16,576]{1,0:T(8,128)(2,1)S(1)} %convert.14), channel_id=1, source_target_pairs={{0,3},{1,4},{2,5},{3,6},{4,7},{5,8},{6,9},{7,10},{8,11},{9,12},{10... | collective-permute-start | bytes 55304
  212.7 15.3 %collective-permute-start.3 = (bf16[16,576]{1,0:T(8,128)(2,1)S(1)}, bf16[16,576]{1,0:T(8,128)(2,1)S(1)}, u32[]{:S(2)}, u32[]{:S(2)}) collective-permute-start(bf16[16,576]{1,0:T(8,128)(2,1)S(1)} %convert.14), channel_id=1, source_target_pairs={{0,4},{1,5},{2,6},{3,7},{4,8},{5,9},{6,10},{7,11},{8,12},{9,13},{1... | collective-permute-start | bytes 55304
  217.6 10.4 %collective-permute-start.4 = (bf16[16,576]{1,0:T(8,128)(2,1)S(1)}, bf16[16,576]{1,0:T(8,128)(2,1)S(1)}, u32[]{:S(2)}, u32[]{:S(2)}) collective-permute-start(bf16[16,576]{1,0:T(8,128)(2,1)S(1)} %convert.14), channel_id=1, source_target_pairs={{0,5},{1,6},{2,7},{3,8},{4,9},{5,10},{6,11},{7,12},{8,13},{9,14},{... | collective-permute-start | bytes 55304
  219.8 8.3 %collective-permute-start.5 = (bf16[16,576]{1,0:T(8,128)(2,1)S(1)}, bf16[16,576]{1,0:T(8,128)(2,1)S(1)}, u32[]{:S(2)}, u32[]{:S(2)}) collective-permute-start(bf16[16,576]{1,0:T(8,128)(2,1)S(1)} %convert.14), channel_id=1, source_target_pairs={{0,6},{1,7},{2,8},{3,9},{4,10},{5,11},{6,12},{7,13},{8,14},{9,15},... | collective-permute-start | bytes 55304
  223.2 4.8 collective-permute-start.6
  229.4 230.8 %copy-start.2 = (bf16[256,1,576]{0,2,1:T(8,128)(2,1)S(1)}, bf16[256,1,576]{0,2,1:T(8,128)(2,1)}, u32[]{:S(2)}) copy-start(bf16[256,1,576]{0,2,1:T(8,128)(2,1)} %param.14) | copy-start | bytes 884740
  229.4 230.8 %copy-start.6 = (f32[256]{0:T(256)S(1)}, f32[256]{0:T(256)}, u32[]{:S(2)}) copy-start(f32[256]{0:T(256)} %param.13) | copy-start | bytes 3076
  280.2 269.0 %copy-start.7 = (f32[1,576]{1,0:T(1,128)S(1)}, f32[1,576]{1,0:T(1,128)}, u32[]{:S(2)}) copy-start(f32[1,576]{1,0:T(1,128)} %param.15) | copy-start | bytes 6916
  280.2 501.2 %all-reduce.9.cloned.1.call-start = ((), (), s32[]{:S(2)}) async-start(), calls=%async_computation.2 | async-start | bytes 786432 | tf_op jit(solution)/shard_map/psum | solution.py:64
  520.7 23.1 %collective-permute-start.10 = (f32[16,576]{1,0:T(8,128)S(1)}, f32[16,576]{1,0:T(8,128)S(1)}, u32[]{:S(2)}, u32[]{:S(2)}) collective-permute-start(f32[16,576]{1,0:T(8,128)S(1)} %fusion.1), channel_id=1, source_target_pairs={{0,3},{1,4},{2,5},{3,6},{4,7},{5,8},{6,9},{7,10},{8,11},{9,12},{10... | collective-permute-start | bytes 110600
  522.0 24.9 %collective-permute-start.11 = (f32[16,576]{1,0:T(8,128)S(1)}, f32[16,576]{1,0:T(8,128)S(1)}, u32[]{:S(2)}, u32[]{:S(2)}) collective-permute-start(f32[16,576]{1,0:T(8,128)S(1)} %fusion.1), channel_id=1, source_target_pairs={{0,4},{1,5},{2,6},{3,7},{4,8},{5,9},{6,10},{7,11},{8,12},{9,13},{1... | collective-permute-start | bytes 110600
  525.5 15.5 %collective-permute-start.15 = (f32[12,576]{1,0:T(8,128)S(1)}, f32[12,576]{1,0:T(8,128)S(1)}, u32[]{:S(2)}, u32[]{:S(2)}) collective-permute-start(f32[12,576]{1,0:T(8,128)S(1)} %slice.11), channel_id=1, source_target_pairs={{0,8},{1,9},{2,10},{3,11},{4,12},{5,13},{6,14},{7,15},{8,16},{9,17... | collective-permute-start | bytes 82952
  532.6 16.7 %collective-permute-start.12 = (f32[16,576]{1,0:T(8,128)S(1)}, f32[16,576]{1,0:T(8,128)S(1)}, u32[]{:S(2)}, u32[]{:S(2)}) collective-permute-start(f32[16,576]{1,0:T(8,128)S(1)} %fusion.1), channel_id=1, source_target_pairs={{0,5},{1,6},{2,7},{3,8},{4,9},{5,10},{6,11},{7,12},{8,13},{9,14},{... | collective-permute-start | bytes 110600
  537.1 12.2 %collective-permute-start.13 = (f32[16,576]{1,0:T(8,128)S(1)}, f32[16,576]{1,0:T(8,128)S(1)}, u32[]{:S(2)}, u32[]{:S(2)}) collective-permute-start(f32[16,576]{1,0:T(8,128)S(1)} %fusion.1), channel_id=1, source_target_pairs={{0,6},{1,7},{2,8},{3,9},{4,10},{5,11},{6,12},{7,13},{8,14},{9,15},... | collective-permute-start | bytes 110600
  541.0 8.2 %collective-permute-start.14 = (f32[16,576]{1,0:T(8,128)S(1)}, f32[16,576]{1,0:T(8,128)S(1)}, u32[]{:S(2)}, u32[]{:S(2)}) collective-permute-start(f32[16,576]{1,0:T(8,128)S(1)} %fusion.1), channel_id=1, source_target_pairs={{0,7},{1,8},{2,9},{3,10},{4,11},{5,12},{6,13},{7,14},{8,15},{9,16}... | collective-permute-start | bytes 110600
  543.9 5.4 collective-permute-start.8
  547.0 3.3 collective-permute-start.9
  551.3 50.8 %copy-start.1 = (f32[384,256]{1,0:T(8,128)S(1)}, f32[384,256]{1,0:T(8,128)}, u32[]{:S(2)}) copy-start(f32[384,256]{1,0:T(8,128)} %all-reduce.7.cloned.1.call-done) | copy-start | bytes 1179652
Sparse Core Ops, SparseCore 0:
  74.2 47.5 reduce-scatter.7
  280.3 179.8 all-reduce.6
  601.6 179.7 all-reduce.8
where the time goes:
time: 790 us
  waiting for transfers between devices  407 us (52%)
  blocking collectives  294 us (37%)
  starting transfers between devices  56.6 us (7%)
  between operations  14.9 us (2%)
  local copies, waits for them, and re-layouts  10 us (1%)
    psum x1, waiting for transfers between devices, body(): pre = lax.psum(partial_pre, ('mp', 'tok'))  180 us
    psum x1, waiting for transfers between devices, body(): latent_grad = lax.psum(contract_cols(error_all, decoder), ('mp', 'tok'))  178 us
    unnamed x2, blocking collectives  118 us
    all_gather x1, blocking collectives, body(): gathered = lax.all_gather(x_rows, 'lat', axis=0, tiled=True)  61.9 us
    unnamed x16, starting transfers between devices  56.5 us
    all_gather x1, blocking collectives, body(): acts_all = lax.all_gather(acts, 'lat', axis=0, tiled=True)  49.4 us
    all_gather x1, blocking collectives, body(): lax.all_gather(error.astype(jnp.bfloat16), 'lat', axis=0, tiled=True)  48.9 us
    reduce_scatter x1, waiting for transfers between devices, body(): lax.psum_scatter(jnp.concatenate([jnp.dot(block, gate_local, preferred_el...  47.7 us
  transfers between devices with their start and end apart: 19, of which 4 were waited for; matrix products, arithmetic and copies ran while one was open for 0% of the time, Pallas kernels for 0%

commit v1 on v0

--- a/solution.py
+++ b/solution.py
@@ -61,7 +61,8 @@
     error = recon + bias_row - acts.astype(jnp.float32)
     error_all = lax.all_gather(error.astype(jnp.bfloat16), "lat", axis=0, tiled=True)
     decoder_grad = contract_rows(codes, error_all)
-    latent_grad = lax.psum(contract_cols(error_all, decoder), ("mp", "tok"))
+    partial = lax.psum(contract_cols(error_all, decoder), "mp")
+    latent_grad = lax.psum(partial, "tok")
     return (error[None], decoder_grad[:, None, :], latent_grad)
 
 

time: 790 us -> 763 us (0.966)
  waiting for transfers between devices: 407 us -> 378 us
    psum x1 -> x2, waiting for transfers between devices: 178 us -> 150 us  [the longest x1 75.6 us: body(): partial = lax.psum(contract_cols(error_all, decoder), 'mp')]
  transfers between devices with their start and end apart: 19 -> 20, of which waited for: 4 -> 5; matrix products, arithmetic and copies ran while one was open for 0% -> 0% of each run, Pallas kernels for 0% -> 0%
where the time goes in v1:
time: 763 us; the launch traced here: 761 us
  waiting for transfers between devices  378 us (50%)
  blocking collectives  294 us (39%)
  starting transfers between devices  56.6 us (7%)
  between operations  14.9 us (2%)
  local copies, waits for them, and re-layouts  10 us (1%)
    psum x1, waiting for transfers between devices, body(): pre = lax.psum(partial_pre, ('mp', 'tok'))  180 us
    unnamed x2, blocking collectives  118 us
    psum x1, waiting for transfers between devices, body(): partial = lax.psum(contract_cols(error_all, decoder), 'mp')  75.6 us
    psum x1, waiting for transfers between devices, body(): latent_grad = lax.psum(partial, 'tok')  74.1 us
    all_gather x1, blocking collectives, body(): gathered = lax.all_gather(x_rows, 'lat', axis=0, tiled=True)  61.9 us
    unnamed x16, starting transfers between devices  56.5 us
    all_gather x1, blocking collectives, body(): acts_all = lax.all_gather(acts, 'lat', axis=0, tiled=True)  49.4 us
    all_gather x1, blocking collectives, body(): lax.all_gather(error.astype(jnp.bfloat16), 'lat', axis=0, tiled=True)  48.9 us
  transfers between devices with their start and end apart: 20, of which 5 were waited for; matrix products, arithmetic and copies ran while one was open for 0% of the time, Pallas kernels for 0%

profile of v1, /device:TPU:1, one launch (start us, length us, event | category | flops | bytes accessed | tf_op | source)
XLA Modules:
  0.0 761.4 jit_solution(12192304775920358979)
XLA Ops:
  8.0 61.9 %all-gather = bf16[1,384,576]{2,0,1:T(2,128)(2,1)S(1)} all-gather(bf16[1,12,576]{2,0,1:T(2,128)(2,1)S(1)} %copy.20), channel_id=2, replica_groups=mesh['mp'=2,'tok'=8,'lat'=32] {'lat'}, dimensions={1}, use_global_device_ids=true | all-gather | bytes 456192 | tf_op jit(solution)/shard_map/all_gather | solution.py:21
  72.1 2.0 copy.25
  74.1 47.7 %reduce-scatter.8.cloned.1.call-done = f32[48,1152]{1,0:T(8,128)} async-done(((f32[384,1152]{1,0:T(8,128)}), f32[48,1152]{1,0:T(8,128)}) %reduce-scatter.8.cloned.1.call-update) | async-done | bytes 221200 | tf_op jit(solution)/shard_map/reduce_scatter | solution.py:26
  122.9 15.4 %all_gather.13 = bf16[384,576]{1,0:T(8,128)(2,1)S(1)} all-gather(bf16[48,576]{1,0:T(8,128)(2,1)S(1)} %fusion.24), channel_id=1, replica_groups=mesh['mp'=2,'tok'=8,'lat'=32] {'tok'}, dimensions={0}, use_global_device_ids=true | all-gather | bytes 497664 | tf_op jit(solution)/shard_map/all_gather | solution.py:39
  138.8 59.0 %fusion = f32[16,576]{1,0:T(8,128)S(1)} fusion(f32[384,576]{1,0:T(8,128)S(1)} %fusion.2), kind=kCustom, calls=%all-reduce-scatter | all-reduce-scatter fusion | flops 294913 | bytes 923648
  197.9 1.7 collective-permute-start
  199.6 2.1 collective-permute-start.1
  201.7 6.0 collective-permute-start.7
  207.7 4.9 collective-permute-start.2
  212.7 4.9 collective-permute-start.3
  217.6 2.1 collective-permute-start.4
  219.8 3.5 collective-permute-start.5
  223.2 2.8 collective-permute-start.6
  226.1 1.3 dynamic-slice.6
  228.1 1.3 concatenate.4
  229.4 49.4 %all-gather.1 = bf16[32,12,576]{2,1,0:T(8,128)(2,1)S(1)} all-gather(bf16[1,12,576]{2,1,0:T(8,128)(2,1)S(1)} %fusion.31), channel_id=1, replica_groups=mesh['mp'=2,'tok'=8,'lat'=32] {'lat'}, dimensions={0}, use_global_device_ids=true | all-gather | bytes 456192 | tf_op jit(solution)/shard_map/all_gather | solution.py:48
  280.2 180.0 %all-reduce.8.cloned.1.call-done = f32[384,256]{1,0:T(8,128)} async-done(((f32[384,256]{1,0:T(8,128)}), f32[384,256]{1,0:T(8,128)}) %all-reduce.8.cloned.1.call-update) | async-done | bytes 393232 | tf_op jit(solution)/shard_map/psum | solution.py:50
  460.2 1.3 fusion.12
  461.6 59.2 %fusion.1 = f32[16,576]{1,0:T(8,128)S(1)} fusion(f32[384,576]{1,0:T(8,128)S(1)} %fusion.12), kind=kCustom, calls=%all-reduce-scatter.1 | all-reduce-scatter fusion | flops 294913 | bytes 923648
  520.7 1.3 collective-permute-start.10
  522.0 3.4 collective-permute-start.11
  525.5 7.0 collective-permute-start.15
  532.6 4.5 collective-permute-start.12
  537.1 3.9 collective-permute-start.13
  541.0 2.9 collective-permute-start.14
  543.9 3.1 collective-permute-start.8
  547.0 2.2 collective-permute-start.9
  551.3 48.9 %all-gather.2 = bf16[32,12,576]{2,1,0:T(8,128)(2,1)S(1)} all-gather(bf16[1,12,576]{2,1,0:T(8,128)(2,1)S(1)} %get-tuple-element.18), channel_id=1, replica_groups=mesh['mp'=2,'tok'=8,'lat'=32] {'lat'}, dimensions={0}, use_global_device_ids=true | all-gather | bytes 456192 | tf_op jit(solution)/shard_map/all_gather | solution.py:62
  601.6 75.6 %all-reduce.10.cloned.1.call-done = f32[384,256]{1,0:T(8,128)} async-done(((f32[384,256]{1,0:T(8,128)}), f32[384,256]{1,0:T(8,128)}) %all-reduce.10.cloned.1.call-update) | async-done | bytes 393232 | tf_op jit(solution)/shard_map/psum | solution.py:64
  677.8 1.2 convolution_bitcast_fusion
  679.0 74.1 %all-reduce.12.cloned.1.call-done = f32[384,256]{1,0:T(8,128)} async-done(((f32[384,256]{1,0:T(8,128)}), f32[384,256]{1,0:T(8,128)}) %all-reduce.12.cloned.1.call-update) | async-done | bytes 393232 | tf_op jit(solution)/shard_map/psum | solution.py:65
  753.1 1.8 copy.30
  (59 shorter events, 10.2 us)
Async XLA Ops:
  7.2 63.5 %copy-start = (bf16[1,576,576]{2,1,0:T(8,128)(2,1)S(1)}, bf16[1,576,576]{2,1,0:T(8,128)(2,1)}, u32[]{:S(2)}) copy-start(bf16[1,576,576]{2,1,0:T(8,128)(2,1)} %param.10) | copy-start | bytes 1990660
  7.2 114.6 %reduce-scatter.8.cloned.1.call-start = ((), (), s32[]{:S(2)}) async-start(), calls=%async_computation.4 | async-start | bytes 1990656 | tf_op jit(solution)/shard_map/reduce_scatter | solution.py:26
  70.0 1.3 copy-start.3
  74.0 64.2 %copy-start.4 = (bf16[1,576,576]{2,1,0:T(8,128)(2,1)S(1)}, bf16[1,576,576]{2,1,0:T(8,128)(2,1)}, u32[]{:S(2)}) copy-start(bf16[1,576,576]{2,1,0:T(8,128)(2,1)} %param.11) | copy-start | bytes 1990660
  74.1 386.2 %all-reduce.8.cloned.1.call-start = ((), (), s32[]{:S(2)}) async-start(), calls=%async_computation.1 | async-start | bytes 786432 | tf_op jit(solution)/shard_map/psum | solution.py:50
  138.8 140.3 %copy-start.5 = (bf16[1,576,256]{2,1,0:T(8,128)(2,1)S(1)}, bf16[1,576,256]{2,1,0:T(8,128)(2,1)}, u32[]{:S(2)}) copy-start(bf16[1,576,256]{2,1,0:T(8,128)(2,1)} %param.12) | copy-start | bytes 884740
  197.9 21.9 %collective-permute-start = (bf16[16,576]{1,0:T(8,128)(2,1)S(1)}, bf16[16,576]{1,0:T(8,128)(2,1)S(1)}, u32[]{:S(2)}, u32[]{:S(2)}) collective-permute-start(bf16[16,576]{1,0:T(8,128)(2,1)S(1)} %convert.14), channel_id=1, source_target_pairs={{0,1},{1,2},{2,3},{3,4},{4,5},{5,6},{6,7},{7,8},{8,9},{9,10},{10,1... | collective-permute-start | bytes 55304
  199.6 23.6 %collective-permute-start.1 = (bf16[16,576]{1,0:T(8,128)(2,1)S(1)}, bf16[16,576]{1,0:T(8,128)(2,1)S(1)}, u32[]{:S(2)}, u32[]{:S(2)}) collective-permute-start(bf16[16,576]{1,0:T(8,128)(2,1)S(1)} %convert.14), channel_id=1, source_target_pairs={{0,2},{1,3},{2,4},{3,5},{4,6},{5,7},{6,8},{7,9},{8,10},{9,11},{10,... | collective-permute-start | bytes 55304
  201.7 15.9 %collective-permute-start.7 = (bf16[12,576]{1,0:T(8,128)(2,1)S(1)}, bf16[12,576]{1,0:T(8,128)(2,1)S(1)}, u32[]{:S(2)}, u32[]{:S(2)}) collective-permute-start(bf16[12,576]{1,0:T(8,128)(2,1)S(1)} %slice.10), channel_id=1, source_target_pairs={{0,8},{1,9},{2,10},{3,11},{4,12},{5,13},{6,14},{7,15},{8,16},{9,17... | collective-permute-start | bytes 41480
  207.7 20.3 %collective-permute-start.2 = (bf16[16,576]{1,0:T(8,128)(2,1)S(1)}, bf16[16,576]{1,0:T(8,128)(2,1)S(1)}, u32[]{:S(2)}, u32[]{:S(2)}) collective-permute-start(bf16[16,576]{1,0:T(8,128)(2,1)S(1)} %convert.14), channel_id=1, source_target_pairs={{0,3},{1,4},{2,5},{3,6},{4,7},{5,8},{6,9},{7,10},{8,11},{9,12},{10... | collective-permute-start | bytes 55304
  212.7 15.3 %collective-permute-start.3 = (bf16[16,576]{1,0:T(8,128)(2,1)S(1)}, bf16[16,576]{1,0:T(8,128)(2,1)S(1)}, u32[]{:S(2)}, u32[]{:S(2)}) collective-permute-start(bf16[16,576]{1,0:T(8,128)(2,1)S(1)} %convert.14), channel_id=1, source_target_pairs={{0,4},{1,5},{2,6},{3,7},{4,8},{5,9},{6,10},{7,11},{8,12},{9,13},{1... | collective-permute-start | bytes 55304
  217.6 10.4 %collective-permute-start.4 = (bf16[16,576]{1,0:T(8,128)(2,1)S(1)}, bf16[16,576]{1,0:T(8,128)(2,1)S(1)}, u32[]{:S(2)}, u32[]{:S(2)}) collective-permute-start(bf16[16,576]{1,0:T(8,128)(2,1)S(1)} %convert.14), channel_id=1, source_target_pairs={{0,5},{1,6},{2,7},{3,8},{4,9},{5,10},{6,11},{7,12},{8,13},{9,14},{... | collective-permute-start | bytes 55304
  219.8 8.3 %collective-permute-start.5 = (bf16[16,576]{1,0:T(8,128)(2,1)S(1)}, bf16[16,576]{1,0:T(8,128)(2,1)S(1)}, u32[]{:S(2)}, u32[]{:S(2)}) collective-permute-start(bf16[16,576]{1,0:T(8,128)(2,1)S(1)} %convert.14), channel_id=1, source_target_pairs={{0,6},{1,7},{2,8},{3,9},{4,10},{5,11},{6,12},{7,13},{8,14},{9,15},... | collective-permute-start | bytes 55304
  223.2 4.8 collective-permute-start.6
  229.4 230.8 %copy-start.2 = (bf16[256,1,576]{0,2,1:T(8,128)(2,1)S(1)}, bf16[256,1,576]{0,2,1:T(8,128)(2,1)}, u32[]{:S(2)}) copy-start(bf16[256,1,576]{0,2,1:T(8,128)(2,1)} %param.14) | copy-start | bytes 884740
  229.4 230.8 %copy-start.6 = (f32[256]{0:T(256)S(1)}, f32[256]{0:T(256)}, u32[]{:S(2)}) copy-start(f32[256]{0:T(256)} %param.13) | copy-start | bytes 3076
  280.2 269.0 %copy-start.7 = (f32[1,576]{1,0:T(1,128)S(1)}, f32[1,576]{1,0:T(1,128)}, u32[]{:S(2)}) copy-start(f32[1,576]{1,0:T(1,128)} %param.15) | copy-start | bytes 6916
  280.2 397.0 %all-reduce.10.cloned.1.call-start = ((), (), s32[]{:S(2)}) async-start(), calls=%async_computation.2 | async-start | bytes 786432 | tf_op jit(solution)/shard_map/psum | solution.py:64
  520.7 23.1 %collective-permute-start.10 = (f32[16,576]{1,0:T(8,128)S(1)}, f32[16,576]{1,0:T(8,128)S(1)}, u32[]{:S(2)}, u32[]{:S(2)}) collective-permute-start(f32[16,576]{1,0:T(8,128)S(1)} %fusion.1), channel_id=1, source_target_pairs={{0,3},{1,4},{2,5},{3,6},{4,7},{5,8},{6,9},{7,10},{8,11},{9,12},{10... | collective-permute-start | bytes 110600
  522.0 24.9 %collective-permute-start.11 = (f32[16,576]{1,0:T(8,128)S(1)}, f32[16,576]{1,0:T(8,128)S(1)}, u32[]{:S(2)}, u32[]{:S(2)}) collective-permute-start(f32[16,576]{1,0:T(8,128)S(1)} %fusion.1), channel_id=1, source_target_pairs={{0,4},{1,5},{2,6},{3,7},{4,8},{5,9},{6,10},{7,11},{8,12},{9,13},{1... | collective-permute-start | bytes 110600
  525.5 15.5 %collective-permute-start.15 = (f32[12,576]{1,0:T(8,128)S(1)}, f32[12,576]{1,0:T(8,128)S(1)}, u32[]{:S(2)}, u32[]{:S(2)}) collective-permute-start(f32[12,576]{1,0:T(8,128)S(1)} %slice.11), channel_id=1, source_target_pairs={{0,8},{1,9},{2,10},{3,11},{4,12},{5,13},{6,14},{7,15},{8,16},{9,17... | collective-permute-start | bytes 82952
  532.6 16.7 %collective-permute-start.12 = (f32[16,576]{1,0:T(8,128)S(1)}, f32[16,576]{1,0:T(8,128)S(1)}, u32[]{:S(2)}, u32[]{:S(2)}) collective-permute-start(f32[16,576]{1,0:T(8,128)S(1)} %fusion.1), channel_id=1, source_target_pairs={{0,5},{1,6},{2,7},{3,8},{4,9},{5,10},{6,11},{7,12},{8,13},{9,14},{... | collective-permute-start | bytes 110600
  537.1 12.2 %collective-permute-start.13 = (f32[16,576]{1,0:T(8,128)S(1)}, f32[16,576]{1,0:T(8,128)S(1)}, u32[]{:S(2)}, u32[]{:S(2)}) collective-permute-start(f32[16,576]{1,0:T(8,128)S(1)} %fusion.1), channel_id=1, source_target_pairs={{0,6},{1,7},{2,8},{3,9},{4,10},{5,11},{6,12},{7,13},{8,14},{9,15},... | collective-permute-start | bytes 110600
  541.0 8.2 %collective-permute-start.14 = (f32[16,576]{1,0:T(8,128)S(1)}, f32[16,576]{1,0:T(8,128)S(1)}, u32[]{:S(2)}, u32[]{:S(2)}) collective-permute-start(f32[16,576]{1,0:T(8,128)S(1)} %fusion.1), channel_id=1, source_target_pairs={{0,7},{1,8},{2,9},{3,10},{4,11},{5,12},{6,13},{7,14},{8,15},{9,16}... | collective-permute-start | bytes 110600
  543.9 5.4 collective-permute-start.8
  547.0 3.3 collective-permute-start.9
  551.3 126.5 %copy-start.1 = (f32[384,256]{1,0:T(8,128)S(1)}, f32[384,256]{1,0:T(8,128)}, u32[]{:S(2)}) copy-start(f32[384,256]{1,0:T(8,128)} %all-reduce.8.cloned.1.call-done) | copy-start | bytes 1179652
  601.5 151.6 %all-reduce.12.cloned.1.call-start = ((), (), s32[]{:S(2)}) async-start(), calls=%async_computation.3 | async-start | bytes 786432 | tf_op jit(solution)/shard_map/psum | solution.py:65
Sparse Core Ops, SparseCore 0:
  74.2 47.5 reduce-scatter.7
  280.3 179.8 all-reduce.7
  601.6 75.4 all-reduce.9
  679.3 73.7 all-reduce.11
